TPU v7x, 128 devices: a whole 4x4x4 slice. The times are simulated.
128 devices in a mesh: lat: 32 (over z, y, core), tp: 4 (over x).
Axes of the slice: x: 4, y: 4, z: 4, core: 2. Of those that a mesh axis runs over, the one named last changes fastest.
Arguments:
- activations: bfloat16 [8192, 7168], P('lat', 'tp'), may hold values from -16 to 16, as said below
- active_blocks: int32 [8192, 2], P('lat'), may hold values from 0 to 31, all different within a row; in each aligned block of 256 rows (0 to 255, 256 to 511, ...) at most 32 rows name the same one
- enc_weight: bfloat16 [7168, 65536], P('tp', 'lat'), may hold values from -0.0625 to 0.0625
- enc_bias: float32 [65536], P('lat'), may hold values from -3 to 3
- dec_weight: bfloat16 [65536, 7168], P('lat', 'tp'), may hold values from -0.125 to 0.125
- dec_bias: float32 [7168], P('tp'), may hold values from -3 to 3
Outputs:
- token_error: float32 [8192], P('lat')
- mean_error: float32 [], replicated
Inputs may be any that keep to these rules, and one draw needn't show every extreme that they name: `active_blocks`: each row names 2 different blocks; among the rows of one index of lat no block is named more than 32 times, and some block is named exactly 32 times. `activations`: real values.
All inputs are finite; a program needn't handle non-finite values.
Results may differ from a plain program's by a relative error of at most 0.005.
Values may be sent and summed in bfloat16 or wider, within the bound.
No kernel may reach another device: no remote copies, remote signals or barrier semaphores. Data moves between devices by JAX's collectives and lax.ppermute only.
A program may use at most 64 MiB of HBM per device.

v0:
```python
import jax
import jax.numpy as jnp
from jax import lax
from jax.experimental import pallas as pl
from jax.experimental.pallas import tpu as pltpu
from jax.sharding import PartitionSpec as P


AXES = ("lat", "tp")
N_Z, N_Y, N_C, N_X = 4, 4, 2, 4
OWNERS = N_Z * N_Y * N_C
TOK = 256
WIDTH = 1792
BLOCK = 2048
SLOTS = 32
CHUNKS = 2
PART = SLOTS // CHUNKS
ROWS = OWNERS * PART
QUARTER = ROWS // N_X


def split_index(index):
    x = index % N_X
    lat = index // N_X
    return lat // (N_Y * N_C), (lat // N_C) % N_Y, lat % N_C, x


def pairs(change):
    out = []
    for index in range(N_Z * N_Y * N_C * N_X):
        z, y, c, x = change(*split_index(index))
        out.append((index, ((z * N_Y + y) * N_C + c) * N_X + x))
    return out


def first(c):
    return 1 + 2 * c


def second(c):
    return 3 - 2 * c


TO_XA = pairs(lambda z, y, c, x: (z, y, c, x ^ first(c)))
TO_XB = pairs(lambda z, y, c, x: (z, y, c, x ^ second(c)))
TO_CORE = pairs(lambda z, y, c, x: (z, y, 1 - c, x))
TO_X = [pairs(lambda z, y, c, x, d=d: (z, y, c, x ^ d)) for d in (1, 2, 3)]
TO_Y = [pairs(lambda z, y, c, x, d=d: (z, y ^ d, c, x)) for d in (1, 2, 3)]
TO_Z = [pairs(lambda z, y, c, x, d=d: (z ^ d, y, c, x)) for d in (1, 2, 3)]


def send(value, table):
    return lax.ppermute(value, AXES, table)


def smem():
    return pl.BlockSpec(memory_space=pltpu.SMEM)


def whole():
    return pl.BlockSpec(memory_space=pltpu.VMEM)


def near_core(value):
    return pltpu.with_memory_space_constraint(value, pltpu.VMEM)


def call(kernel, outs, args, flops, local=(), scalars=0):
    moved = sum(a.size * a.dtype.itemsize for a in args) // 4
    args = [near_core(a) if i in local else a for i, a in enumerate(args)]
    return pl.pallas_call(
        kernel,
        in_specs=[smem()] * scalars + [whole()] * (len(args) - scalars),
        out_specs=[whole()] * len(outs),
        out_shape=[jax.ShapeDtypeStruct(shape, dtype) for shape, dtype in outs],
        cost_estimate=pl.CostEstimate(flops=flops, transcendentals=0, bytes_accessed=moved),
    )(*args)


def lane_sums(values):
    acc = values[:, :128]
    for start in range(128, values.shape[1], 128):
        acc = acc + values[:, start:start + 128]
    return jnp.sum(acc.T, axis=0, keepdims=True)


def code_kernel(ids_ref, code_ref):
    block = lax.broadcasted_iota(jnp.int32, (OWNERS, TOK), 0)
    one0 = jnp.where(ids_ref[0:1, :] == block, 1.0, 0.0)
    one1 = jnp.where(ids_ref[1:2, :] == block, 1.0, 0.0)
    before = lax.broadcasted_iota(jnp.int32, (TOK, TOK), 0) < lax.broadcasted_iota(jnp.int32, (TOK, TOK), 1)
    before = jnp.where(before, 1.0, 0.0).astype(jnp.bfloat16)
    count0 = jnp.dot(one0.astype(jnp.bfloat16), before, preferred_element_type=jnp.float32)
    count1 = jnp.dot(one1.astype(jnp.bfloat16), before, preferred_element_type=jnp.float32)
    count1 = count1 + jnp.sum(one0, axis=1, keepdims=True)
    rank0 = jnp.sum(one0 * count0, axis=0, keepdims=True)
    rank1 = jnp.sum(one1 * count1, axis=0, keepdims=True)
    code_ref[0:1, :] = ids_ref[0:1, :] * SLOTS + rank0.astype(jnp.int32)
    code_ref[1:2, :] = ids_ref[1:2, :] * SLOTS + rank1.astype(jnp.int32)


def codes(ids):
    return call(code_kernel, [((2, TOK), jnp.int32)], [ids], 2**24)[0]


def picks(code_ref, chunk):
    row = lax.broadcasted_iota(jnp.int32, (ROWS, 1), 0)
    want = row // PART * SLOTS + chunk * PART + row % PART
    hit = (code_ref[0:1, :] == want) | (code_ref[1:2, :] == want)
    return jnp.where(hit, 1.0, 0.0).astype(jnp.bfloat16)


def pack(chunk, activations, code, dec_bias):
    def kernel(act_ref, code_ref, bias_ref, out_ref):
        centred = (act_ref[...].astype(jnp.float32) - bias_ref[...]).astype(jnp.bfloat16)
        rows = jnp.dot(picks(code_ref, chunk), centred, preferred_element_type=jnp.float32)
        out_ref[...] = rows.astype(jnp.bfloat16).reshape(OWNERS, PART, WIDTH)

    return call(kernel, [((OWNERS, PART, WIDTH), jnp.bfloat16)], [activations, code, dec_bias], 2 * ROWS * TOK * WIDTH)[0]


def norm_sums(activations):
    def kernel(act_ref, out_ref):
        values = act_ref[...].astype(jnp.float32)
        out_ref[...] = lane_sums(values * values)

    return call(kernel, [((1, TOK), jnp.float32)], [activations], 2**20)[0]


def quarters(meta):
    index = meta[0]
    x, c = index % N_X, (index // N_X) % N_C
    return [pl.multiple_of((x ^ d) * QUARTER, QUARTER) for d in (0, second(c), first(c), 2)]


def encode(meta, rows, weight, tile=512):
    def kernel(meta_ref, rows_ref, weight_ref, own_ref, near_ref, away_ref, part_ref):
        own, near, away, far = quarters(meta_ref)
        part = jnp.dot(rows_ref[...].reshape(ROWS, WIDTH), weight_ref[...], preferred_element_type=jnp.float32)
        part_ref[...] = part.astype(jnp.bfloat16)
        own_ref[...] = part_ref[pl.ds(own, QUARTER), :]
        near_ref[...] = part_ref[pl.ds(near, QUARTER), :]
        away_ref[0:QUARTER, :] = part_ref[pl.ds(away, QUARTER), :]
        away_ref[QUARTER:, :] = part_ref[pl.ds(far, QUARTER), :]

    outs = [QUARTER, QUARTER, 2 * QUARTER]
    return pl.pallas_call(
        kernel,
        grid=(BLOCK // tile,),
        in_specs=[smem(), whole(), pl.BlockSpec((WIDTH, tile), lambda j: (0, j))],
        out_specs=[pl.BlockSpec((count, tile), lambda j: (0, j)) for count in outs],
        out_shape=[jax.ShapeDtypeStruct((count, BLOCK), jnp.bfloat16) for count in outs],
        scratch_shapes=[pltpu.VMEM((ROWS, tile), jnp.bfloat16)],
        cost_estimate=pl.CostEstimate(flops=2 * ROWS * WIDTH * BLOCK, transcendentals=0, bytes_accessed=2 * WIDTH * BLOCK),
        name="encode",
    )(meta, near_core(rows), weight)


def join(near_part, got):
    def kernel(near_ref, got_ref, out_ref):
        total = near_ref[...].astype(jnp.float32) + got_ref[QUARTER:, :].astype(jnp.float32)
        out_ref[...] = total.astype(jnp.bfloat16)

    return call(kernel, [((QUARTER, BLOCK), jnp.bfloat16)], [near_part, got], 2**18, local=(1,))[0]


def activate(own_part, got, rest, enc_bias):
    def kernel(own_ref, got_ref, rest_ref, bias_ref, out_ref):
        pre = own_ref[...].astype(jnp.float32) + got_ref[0:QUARTER, :].astype(jnp.float32)
        pre = pre + rest_ref[...].astype(jnp.float32) + bias_ref[...]
        out_ref[...] = jnp.maximum(pre, 0.0).astype(jnp.bfloat16)

    return call(kernel, [((QUARTER, BLOCK), jnp.bfloat16)], [own_part, got, rest, enc_bias], 2**19, local=(1, 2))[0]


def decode(meta, own, others, weight, tile=256):
    def kernel(meta_ref, own_ref, near_ref, away_ref, far_ref, weight_ref, out_ref, rows_ref):
        @pl.when(pl.program_id(0) == 0)
        def _():
            for start, part_ref in zip(quarters(meta_ref), (own_ref, near_ref, away_ref, far_ref)):
                rows_ref[pl.ds(start, QUARTER), :] = part_ref[...]

        rows = jnp.dot(rows_ref[...], weight_ref[...], preferred_element_type=jnp.float32)
        out_ref[...] = rows.astype(jnp.bfloat16).reshape(OWNERS, PART, tile)

    return pl.pallas_call(
        kernel,
        grid=(WIDTH // tile,),
        in_specs=[smem()] + [whole()] * 4 + [pl.BlockSpec((BLOCK, tile), lambda j: (0, j))],
        out_specs=pl.BlockSpec((OWNERS, PART, tile), lambda j: (0, 0, j)),
        out_shape=jax.ShapeDtypeStruct((OWNERS, PART, WIDTH), jnp.bfloat16),
        scratch_shapes=[pltpu.VMEM((ROWS, BLOCK), jnp.bfloat16)],
        cost_estimate=pl.CostEstimate(flops=2 * ROWS * WIDTH * BLOCK, transcendentals=0, bytes_accessed=2 * WIDTH * BLOCK),
        name="decode",
    )(meta, own, *[near_core(a) for a in others], weight)


def collect(chunk, code_ref, rows_ref):
    return lax.dot_general(
        picks(code_ref, chunk), rows_ref[...].reshape(ROWS, WIDTH), (((0,), (0,)), ((), ())), preferred_element_type=jnp.float32
    )


def collect_rows(chunk, code, rows, base):
    def kernel(code_ref, rows_ref, base_ref, out_ref):
        out_ref[...] = base_ref[...] + collect(chunk, code_ref, rows_ref)

    return call(kernel, [((TOK, WIDTH), jnp.float32)], [code, rows, base], 2 * ROWS * TOK * WIDTH)[0]


def finish(chunk, activations, code, rows, base):
    def kernel(act_ref, code_ref, rows_ref, base_ref, out_ref):
        recon = base_ref[...] + collect(chunk, code_ref, rows_ref)
        diff = act_ref[...].astype(jnp.float32) - recon
        out_ref[...] = lane_sums(diff * diff)

    return call(kernel, [((1, TOK), jnp.float32)], [activations, code, rows, base], 2 * ROWS * TOK * WIDTH, local=(2,))[0]


def sum_tp(value):
    one, two, three = (send(value, table) for table in TO_X)
    return (value + two) + (one + three)


def exchange(rows):
    return lax.all_to_all(rows, "lat", split_axis=0, concat_axis=0, tiled=True)


def steps(activations, active_blocks, enc_weight, enc_bias, dec_weight, dec_bias):
    meta = (lax.axis_index("lat") * N_X + lax.axis_index("tp")).astype(jnp.int32).reshape(1)
    bias_row = dec_bias.reshape(1, WIDTH)
    code = codes(active_blocks.T)

    def forward(n):
        rows = pack(n, activations, code, bias_row)
        rows = exchange(rows)
        own_part, near_part, away_part = encode(meta, rows, enc_weight)
        got = send(away_part, TO_XA)
        near_sum = join(near_part, got)
        rest = send(near_sum, TO_XB)
        mine = activate(own_part, got, rest, enc_bias.reshape(1, BLOCK))
        near = send(mine, TO_XB)
        away = send(mine, TO_XA)
        far = send(near, TO_XA)
        rows = decode(meta, mine, (near, away, far), dec_weight)
        return exchange(rows)

    back = [forward(n) for n in range(CHUNKS)]
    norms = sum_tp(norm_sums(activations)) + 1e-6
    recon = bias_row
    for n in range(CHUNKS - 1):
        recon = collect_rows(n, code, back[n], recon)
    partial = finish(CHUNKS - 1, activations, code, back[-1], recon)
    squares = sum_tp(partial)
    token_error = (squares / norms).reshape(TOK)
    total = token_error[:128] + token_error[128:]
    total = total + send(total, TO_CORE)
    for tables in (TO_Y, TO_Z):
        one, two, three = (send(total, table) for table in tables)
        total = (total + two) + (one + three)
    mean_error = jnp.sum(total) / (TOK * OWNERS)
    return (token_error, mean_error)


def solution(mesh):
    in_specs = (P("lat", "tp"), P("lat", None), P("tp", "lat"), P("lat"), P("lat", "tp"), P("tp"))
    out_specs = (P("lat"), P())
    return jax.shard_map(steps, mesh=mesh, in_specs=in_specs, out_specs=out_specs, check_vma=False)
```

profile of v0, /device:TPU:1, one launch (start us, length us, event | category | flops | bytes accessed | tf_op | source)
XLA Modules:
  0.0 232.0 jit_solution(12672267179126470474)
XLA Ops:
  3.4 3.2 %shard_map.81 = bf16[32,16,1792]{2,1,0:T(8,128)(2,1)} custom-call(bf16[256,1792]{1,0:T(8,128)(2,1)} %act_ref.7, s32[2,256]{1,0:T(2,128)} %shard_map.77.code_ref, f32[1,1792]{1,0:T(1,128)} %reshape.21.bias_ref.base_ref), custom_call_target="tpu_custom_call" | custom-call | flops 469762048 | bytes 231680 | tf_op jit(solution)/shard_map/pallas_call | solution.py:71
  6.5 9.6 %all-to-all-start.2 = ((bf16[32,16,1792]{2,1,0:T(8,128)(2,1)}), bf16[32,16,1792]{2,1,0:T(8,128)(2,1)S(1)}, u32[]{:S(2)}, u32[]{:S(2)}) async-start(bf16[32,16,1792]{2,1,0:T(8,128)(2,1)} %shard_map.81), calls=%async_computation.2 | async-start | bytes 3670016 | tf_op jit(solution)/shard_map/all_to_all | solution.py:226
  16.1 3.1 %shard_map.78 = bf16[32,16,1792]{2,1,0:T(8,128)(2,1)} custom-call(bf16[256,1792]{1,0:T(8,128)(2,1)} %act_ref.7, s32[2,256]{1,0:T(2,128)} %shard_map.77.code_ref, f32[1,1792]{1,0:T(1,128)} %reshape.21.bias_ref.base_ref), custom_call_target="tpu_custom_call" | custom-call | flops 469762048 | bytes 231680 | tf_op jit(solution)/shard_map/pallas_call | solution.py:71
  19.2 22.7 %all-to-all-done.2.rows_ref = bf16[32,16,1792]{2,1,0:T(8,128)(2,1)S(1)} async-done(((bf16[32,16,1792]{2,1,0:T(8,128)(2,1)}), bf16[32,16,1792]{2,1,0:T(8,128)(2,1)S(1)}, u32[]{:S(2)}, u32[]{:S(2)}) %all-to-all-start.2) | async-done | bytes 1835040 | tf_op jit(solution)/shard_map/all_to_all | solution.py:226
  41.9 5.8 %all-to-all-start = ((bf16[32,16,1792]{2,1,0:T(8,128)(2,1)}), bf16[32,16,1792]{2,1,0:T(8,128)(2,1)}, u32[]{:S(2)}, u32[]{:S(2)}) async-start(bf16[32,16,1792]{2,1,0:T(8,128)(2,1)} %shard_map.78), calls=%async_computation | async-start | bytes 3670016 | tf_op jit(solution)/shard_map/all_to_all | solution.py:226
  47.7 7.6 %encode.3 = (bf16[128,2048]{1,0:T(8,128)(2,1)}, bf16[128,2048]{1,0:T(8,128)(2,1)}, bf16[256,2048]{1,0:T(8,128)(2,1)}) custom-call(s32[1]{0:T(128)} %bitcast.1.meta_ref, bf16[32,16,1792]{2,1,0:T(8,128)(2,1)S(1)} %all-to-all-done.2.rows_ref, bf16[1792,2048]{1,0:T(8,128)(2,1)} %weight_ref.6), custom_call_target="tpu_custom_call" | custom-call | flops 3758096384 | bytes 7340032 | tf_op jit(solution)/shard_map/encode/pallas_call | solution.py:147
  55.3 2.5 %collective-permute-start.5 = (bf16[256,2048]{1,0:T(8,128)(2,1)}, bf16[256,2048]{1,0:T(8,128)(2,1)S(1)}, u32[]{:S(2)}, u32[]{:S(2)}) collective-permute-start(bf16[256,2048]{1,0:T(8,128)(2,1)} %get-tuple-element.12), channel_id=1, source_target_pairs={{0,1},{1,0},{2,3},{3,2},{4,7},{5,6},{6,5},{7,4},{8,9},{9,8},{10,11... | collective-permute-start | bytes 3145736 | tf_op jit(solution)/shard_map/ppermute | solution.py:53
  57.7 12.6 %collective-permute-done.5.got_ref = bf16[256,2048]{1,0:T(8,128)(2,1)S(1)} collective-permute-done((bf16[256,2048]{1,0:T(8,128)(2,1)}, bf16[256,2048]{1,0:T(8,128)(2,1)S(1)}, u32[]{:S(2)}, u32[]{:S(2)}) %collective-permute-start.5) | collective-permute-done | bytes 1048608 | tf_op jit(solution)/shard_map/ppermute | solution.py:53
  73.7 8.2 %encode.2 = (bf16[128,2048]{1,0:T(8,128)(2,1)}, bf16[128,2048]{1,0:T(8,128)(2,1)}, bf16[256,2048]{1,0:T(8,128)(2,1)}) custom-call(s32[1]{0:T(128)} %bitcast.1.meta_ref, bf16[32,16,1792]{2,1,0:T(8,128)(2,1)} %all-to-all-done.rows_ref, bf16[1792,2048]{1,0:T(8,128)(2,1)} %weight_ref.6), custom_call_target="tpu_custom_call" | custom-call | flops 3758096384 | bytes 7340032 | tf_op jit(solution)/shard_map/encode/pallas_call | solution.py:147
  81.8 2.3 collective-permute-start
  88.7 12.9 %collective-permute-done.7.near_ref = bf16[128,2048]{1,0:T(8,128)(2,1)S(1)} collective-permute-done((bf16[128,2048]{1,0:T(8,128)(2,1)}, bf16[128,2048]{1,0:T(8,128)(2,1)S(1)}, u32[]{:S(2)}, u32[]{:S(2)}) %collective-permute-start.7) | collective-permute-done | bytes 524320 | tf_op jit(solution)/shard_map/ppermute | solution.py:53
  104.2 3.9 %collective-permute-done.8.away_ref = bf16[128,2048]{1,0:T(8,128)(2,1)S(1)} collective-permute-done((bf16[128,2048]{1,0:T(8,128)(2,1)}, bf16[128,2048]{1,0:T(8,128)(2,1)S(1)}, u32[]{:S(2)}, u32[]{:S(2)}) %collective-permute-start.8) | collective-permute-done | bytes 524320 | tf_op jit(solution)/shard_map/ppermute | solution.py:53
  108.1 8.2 %collective-permute-done.9.far_ref = bf16[128,2048]{1,0:T(8,128)(2,1)S(1)} collective-permute-done((bf16[128,2048]{1,0:T(8,128)(2,1)S(1)}, bf16[128,2048]{1,0:T(8,128)(2,1)S(1)}, u32[]{:S(2)}, u32[]{:S(2)}) %collective-permute-start.9) | collective-permute-done | bytes 524320 | tf_op jit(solution)/shard_map/ppermute | solution.py:53
  116.4 9.2 %decode.3 = bf16[32,16,1792]{2,1,0:T(8,128)(2,1)} custom-call(s32[1]{0:T(128)} %bitcast.1.meta_ref, bf16[128,2048]{1,0:T(8,128)(2,1)} %shard_map.83.own_ref, bf16[128,2048]{1,0:T(8,128)(2,1)S(1)} %collective-permute-done.7.near_ref, bf16[128,2048]{1,0:T(8,128)(2,1)S(1)} %collective-permute-done.8.away_ref, ...), custom_call_target="tpu_custom_call" | custom-call | flops 3758096384 | bytes 7340032 | tf_op jit(solution)/shard_map/decode/pallas_call | solution.py:186
  125.5 12.8 %all-to-all-start.3 = ((bf16[32,16,1792]{2,1,0:T(8,128)(2,1)}), bf16[32,16,1792]{2,1,0:T(8,128)(2,1)}, u32[]{:S(2)}, u32[]{:S(2)}) async-start(bf16[32,16,1792]{2,1,0:T(8,128)(2,1)} %decode.3), calls=%async_computation.3 | async-start | bytes 3670016 | tf_op jit(solution)/shard_map/all_to_all | solution.py:226
  141.3 12.2 %collective-permute-done.2.near_ref = bf16[128,2048]{1,0:T(8,128)(2,1)S(1)} collective-permute-done((bf16[128,2048]{1,0:T(8,128)(2,1)}, bf16[128,2048]{1,0:T(8,128)(2,1)S(1)}, u32[]{:S(2)}, u32[]{:S(2)}) %collective-permute-start.2) | collective-permute-done | bytes 524320 | tf_op jit(solution)/shard_map/ppermute | solution.py:53
  155.2 7.5 %collective-permute-done.4.far_ref = bf16[128,2048]{1,0:T(8,128)(2,1)S(1)} collective-permute-done((bf16[128,2048]{1,0:T(8,128)(2,1)S(1)}, bf16[128,2048]{1,0:T(8,128)(2,1)S(1)}, u32[]{:S(2)}, u32[]{:S(2)}) %collective-permute-start.4) | collective-permute-done | bytes 524320 | tf_op jit(solution)/shard_map/ppermute | solution.py:53
  162.7 9.2 %decode.2 = bf16[32,16,1792]{2,1,0:T(8,128)(2,1)} custom-call(s32[1]{0:T(128)} %bitcast.1.meta_ref, bf16[128,2048]{1,0:T(8,128)(2,1)} %shard_map.80.own_ref, bf16[128,2048]{1,0:T(8,128)(2,1)S(1)} %collective-permute-done.2.near_ref, bf16[128,2048]{1,0:T(8,128)(2,1)S(1)} %collective-permute-done.3.away_ref, ...), custom_call_target="tpu_custom_call" | custom-call | flops 3758096384 | bytes 7340032 | tf_op jit(solution)/shard_map/decode/pallas_call | solution.py:186
  171.9 9.7 %all-to-all-start.1 = ((bf16[32,16,1792]{2,1,0:T(8,128)(2,1)}), bf16[32,16,1792]{2,1,0:T(8,128)(2,1)S(1)}, u32[]{:S(2)}, u32[]{:S(2)}) async-start(bf16[32,16,1792]{2,1,0:T(8,128)(2,1)} %decode.2), calls=%async_computation.1 | async-start | bytes 3670016 | tf_op jit(solution)/shard_map/all_to_all | solution.py:226
  186.9 3.5 %shard_map.84.base_ref = f32[256,1792]{1,0:T(8,128)} custom-call(s32[2,256]{1,0:T(2,128)} %shard_map.77.code_ref, bf16[32,16,1792]{2,1,0:T(8,128)(2,1)} %all-to-all-done.3.rows_ref, f32[1,1792]{1,0:T(1,128)} %reshape.21.bias_ref.base_ref), custom_call_target="tpu_custom_call" | custom-call | flops 469762048 | bytes 461056 | tf_op jit(solution)/shard_map/pallas_call | solution.py:71
  190.3 17.1 %all-to-all-done.1.rows_ref = bf16[32,16,1792]{2,1,0:T(8,128)(2,1)S(1)} async-done(((bf16[32,16,1792]{2,1,0:T(8,128)(2,1)}), bf16[32,16,1792]{2,1,0:T(8,128)(2,1)S(1)}, u32[]{:S(2)}, u32[]{:S(2)}) %all-to-all-start.1) | async-done | bytes 1835040 | tf_op jit(solution)/shard_map/all_to_all | solution.py:226
  207.4 3.2 %shard_map.85 = f32[1,256]{1,0:T(1,128)} custom-call(bf16[256,1792]{1,0:T(8,128)(2,1)} %act_ref.7, s32[2,256]{1,0:T(2,128)} %shard_map.77.code_ref, bf16[32,16,1792]{2,1,0:T(8,128)(2,1)S(1)} %all-to-all-done.1.rows_ref, f32[256,1792]{1,0:T(8,128)} %shard_map.84.base_ref), custom_call_target="tpu_custom_call" | custom-call | flops 469762048 | bytes 1147392 | tf_op jit(solution)/shard_map/pallas_call | solution.py:71
  216.5 3.2 %collective-permute-start.16 = (f32[128]{0:T(128)S(1)}, f32[128]{0:T(128)S(1)}, u32[]{:S(2)}, u32[]{:S(2)}) collective-permute-start(f32[128]{0:T(128)S(1)} %fusion), channel_id=1, source_target_pairs={{0,4},{1,5},{2,6},{3,7},{4,0},{5,1},{6,2},{7,3},{8,12},{9,13},{10,... | collective-permute-start | bytes 1544 | tf_op jit(solution)/shard_map/ppermute | solution.py:53
  220.6 3.2 %collective-permute-start.19 = (f32[128]{0:T(128)S(1)}, f32[128]{0:T(128)S(1)}, u32[]{:S(2)}, u32[]{:S(2)}) collective-permute-start(f32[128]{0:T(128)S(1)} %fusion.1), channel_id=1, source_target_pairs={{0,24},{1,25},{2,26},{3,27},{4,28},{5,29},{6,30},{7,31},{8,16},{9,... | collective-permute-start | bytes 1544 | tf_op jit(solution)/shard_map/ppermute | solution.py:53
  (58 shorter events, 36.3 us)
Async XLA Ops:
  6.5 35.4 %all-to-all-start.2 = ((bf16[32,16,1792]{2,1,0:T(8,128)(2,1)}), bf16[32,16,1792]{2,1,0:T(8,128)(2,1)S(1)}, u32[]{:S(2)}, u32[]{:S(2)}) async-start(bf16[32,16,1792]{2,1,0:T(8,128)(2,1)} %shard_map.81), calls=%async_computation.2 | async-start | bytes 3670016 | tf_op jit(solution)/shard_map/all_to_all | solution.py:226
  41.9 31.8 %all-to-all-start = ((bf16[32,16,1792]{2,1,0:T(8,128)(2,1)}), bf16[32,16,1792]{2,1,0:T(8,128)(2,1)}, u32[]{:S(2)}, u32[]{:S(2)}) async-start(bf16[32,16,1792]{2,1,0:T(8,128)(2,1)} %shard_map.78), calls=%async_computation | async-start | bytes 3670016 | tf_op jit(solution)/shard_map/all_to_all | solution.py:226
  55.3 15.1 %collective-permute-start.5 = (bf16[256,2048]{1,0:T(8,128)(2,1)}, bf16[256,2048]{1,0:T(8,128)(2,1)S(1)}, u32[]{:S(2)}, u32[]{:S(2)}) collective-permute-start(bf16[256,2048]{1,0:T(8,128)(2,1)} %get-tuple-element.12), channel_id=1, source_target_pairs={{0,1},{1,0},{2,3},{3,2},{4,7},{5,6},{6,5},{7,4},{8,9},{9,8},{10,11... | collective-permute-start | bytes 3145736 | tf_op jit(solution)/shard_map/ppermute | solution.py:53
  73.3 10.8 %collective-permute-start.6 = (bf16[128,2048]{1,0:T(8,128)(2,1)}, bf16[128,2048]{1,0:T(8,128)(2,1)S(1)}, u32[]{:S(2)}, u32[]{:S(2)}) collective-permute-start(bf16[128,2048]{1,0:T(8,128)(2,1)} %shard_map.82), channel_id=1, source_target_pairs={{0,3},{1,2},{2,1},{3,0},{4,5},{5,4},{6,7},{7,6},{8,11},{9,10},{10,... | collective-permute-start | bytes 1572872 | tf_op jit(solution)/shard_map/ppermute | solution.py:53
  81.8 20.2 %collective-permute-start = (bf16[256,2048]{1,0:T(8,128)(2,1)}, bf16[256,2048]{1,0:T(8,128)(2,1)S(1)}, u32[]{:S(2)}, u32[]{:S(2)}) collective-permute-start(bf16[256,2048]{1,0:T(8,128)(2,1)} %get-tuple-element.9), channel_id=1, source_target_pairs={{0,1},{1,0},{2,3},{3,2},{4,7},{5,6},{6,5},{7,4},{8,9},{9,8},{10,11... | collective-permute-start | bytes 3145736 | tf_op jit(solution)/shard_map/ppermute | solution.py:53
  87.4 14.2 %collective-permute-start.7 = (bf16[128,2048]{1,0:T(8,128)(2,1)}, bf16[128,2048]{1,0:T(8,128)(2,1)S(1)}, u32[]{:S(2)}, u32[]{:S(2)}) collective-permute-start(bf16[128,2048]{1,0:T(8,128)(2,1)} %shard_map.83.own_ref), channel_id=1, source_target_pairs={{0,3},{1,2},{2,1},{3,0},{4,5},{5,4},{6,7},{7,6},{8,11},{9,10},{10,... | collective-permute-start | bytes 1572872 | tf_op jit(solution)/shard_map/ppermute | solution.py:53
  88.1 20.0 %collective-permute-start.8 = (bf16[128,2048]{1,0:T(8,128)(2,1)}, bf16[128,2048]{1,0:T(8,128)(2,1)S(1)}, u32[]{:S(2)}, u32[]{:S(2)}) collective-permute-start(bf16[128,2048]{1,0:T(8,128)(2,1)} %shard_map.83.own_ref), channel_id=1, source_target_pairs={{0,1},{1,0},{2,3},{3,2},{4,7},{5,6},{6,5},{7,4},{8,9},{9,8},{10,11... | collective-permute-start | bytes 1572872 | tf_op jit(solution)/shard_map/ppermute | solution.py:53
  101.6 14.8 %collective-permute-start.9 = (bf16[128,2048]{1,0:T(8,128)(2,1)S(1)}, bf16[128,2048]{1,0:T(8,128)(2,1)S(1)}, u32[]{:S(2)}, u32[]{:S(2)}) collective-permute-start(bf16[128,2048]{1,0:T(8,128)(2,1)S(1)} %collective-permute-done.7.near_ref), channel_id=1, source_target_pairs={{0,1},{1,0},{2,3},{3,2},{4,7},{5,6},{6,5},{7,4},{8,9},{9,8},{10,11... | collective-permute-start | bytes 1572872 | tf_op jit(solution)/shard_map/ppermute | solution.py:53
  104.0 34.4 %collective-permute-start.1 = (bf16[128,2048]{1,0:T(8,128)(2,1)}, bf16[128,2048]{1,0:T(8,128)(2,1)S(1)}, u32[]{:S(2)}, u32[]{:S(2)}) collective-permute-start(bf16[128,2048]{1,0:T(8,128)(2,1)} %shard_map.79), channel_id=1, source_target_pairs={{0,3},{1,2},{2,1},{3,0},{4,5},{5,4},{6,7},{7,6},{8,11},{9,10},{10,... | collective-permute-start | bytes 1572872 | tf_op jit(solution)/shard_map/ppermute | solution.py:53
  125.5 46.4 %all-to-all-start.3 = ((bf16[32,16,1792]{2,1,0:T(8,128)(2,1)}), bf16[32,16,1792]{2,1,0:T(8,128)(2,1)}, u32[]{:S(2)}, u32[]{:S(2)}) async-start(bf16[32,16,1792]{2,1,0:T(8,128)(2,1)} %decode.3), calls=%async_computation.3 | async-start | bytes 3670016 | tf_op jit(solution)/shard_map/all_to_all | solution.py:226
  140.5 13.0 %collective-permute-start.2 = (bf16[128,2048]{1,0:T(8,128)(2,1)}, bf16[128,2048]{1,0:T(8,128)(2,1)S(1)}, u32[]{:S(2)}, u32[]{:S(2)}) collective-permute-start(bf16[128,2048]{1,0:T(8,128)(2,1)} %shard_map.80.own_ref), channel_id=1, source_target_pairs={{0,3},{1,2},{2,1},{3,0},{4,5},{5,4},{6,7},{7,6},{8,11},{9,10},{10,... | collective-permute-start | bytes 1572872 | tf_op jit(solution)/shard_map/ppermute | solution.py:53
  140.5 14.7 %collective-permute-start.3 = (bf16[128,2048]{1,0:T(8,128)(2,1)}, bf16[128,2048]{1,0:T(8,128)(2,1)S(1)}, u32[]{:S(2)}, u32[]{:S(2)}) collective-permute-start(bf16[128,2048]{1,0:T(8,128)(2,1)} %shard_map.80.own_ref), channel_id=1, source_target_pairs={{0,1},{1,0},{2,3},{3,2},{4,7},{5,6},{6,5},{7,4},{8,9},{9,8},{10,11... | collective-permute-start | bytes 1572872 | tf_op jit(solution)/shard_map/ppermute | solution.py:53
  153.5 9.2 %collective-permute-start.4 = (bf16[128,2048]{1,0:T(8,128)(2,1)S(1)}, bf16[128,2048]{1,0:T(8,128)(2,1)S(1)}, u32[]{:S(2)}, u32[]{:S(2)}) collective-permute-start(bf16[128,2048]{1,0:T(8,128)(2,1)S(1)} %collective-permute-done.2.near_ref), channel_id=1, source_target_pairs={{0,1},{1,0},{2,3},{3,2},{4,7},{5,6},{6,5},{7,4},{8,9},{9,8},{10,11... | collective-permute-start | bytes 1572872 | tf_op jit(solution)/shard_map/ppermute | solution.py:53
  171.9 35.5 %all-to-all-start.1 = ((bf16[32,16,1792]{2,1,0:T(8,128)(2,1)}), bf16[32,16,1792]{2,1,0:T(8,128)(2,1)S(1)}, u32[]{:S(2)}, u32[]{:S(2)}) async-start(bf16[32,16,1792]{2,1,0:T(8,128)(2,1)} %decode.2), calls=%async_computation.1 | async-start | bytes 3670016 | tf_op jit(solution)/shard_map/all_to_all | solution.py:226
  183.6 28.4 %collective-permute-start.13 = (f32[1,256]{1,0:T(1,128)}, f32[1,256]{1,0:T(1,128)S(1)}, u32[]{:S(2)}, u32[]{:S(2)}) collective-permute-start(f32[1,256]{1,0:T(1,128)} %shard_map.86), channel_id=1, source_target_pairs={{0,2},{1,3},{2,0},{3,1},{4,6},{5,7},{6,4},{7,5},{8,10},{9,11},{10,... | collective-permute-start | bytes 3080 | tf_op jit(solution)/shard_map/ppermute | solution.py:53
  183.9 30.0 %collective-permute-start.14 = (f32[1,256]{1,0:T(1,128)}, f32[1,256]{1,0:T(1,128)S(1)}, u32[]{:S(2)}, u32[]{:S(2)}) collective-permute-start(f32[1,256]{1,0:T(1,128)} %shard_map.86), channel_id=1, source_target_pairs={{0,1},{1,0},{2,3},{3,2},{4,5},{5,4},{6,7},{7,6},{8,9},{9,8},{10,11... | collective-permute-start | bytes 3080 | tf_op jit(solution)/shard_map/ppermute | solution.py:53
  185.0 28.9 %collective-permute-start.15 = (f32[1,256]{1,0:T(1,128)}, f32[1,256]{1,0:T(1,128)S(1)}, u32[]{:S(2)}, u32[]{:S(2)}) collective-permute-start(f32[1,256]{1,0:T(1,128)} %shard_map.86), channel_id=1, source_target_pairs={{0,3},{1,2},{2,1},{3,0},{4,7},{5,6},{6,5},{7,4},{8,11},{9,10},{10,... | collective-permute-start | bytes 3080 | tf_op jit(solution)/shard_map/ppermute | solution.py:53
  210.6 4.1 %collective-permute-start.10 = (f32[1,256]{1,0:T(1,128)}, f32[1,256]{1,0:T(1,128)S(1)}, u32[]{:S(2)}, u32[]{:S(2)}) collective-permute-start(f32[1,256]{1,0:T(1,128)} %shard_map.85), channel_id=1, source_target_pairs={{0,2},{1,3},{2,0},{3,1},{4,6},{5,7},{6,4},{7,5},{8,10},{9,11},{10,... | collective-permute-start | bytes 3080 | tf_op jit(solution)/shard_map/ppermute | solution.py:53
  210.9 3.9 %collective-permute-start.11 = (f32[1,256]{1,0:T(1,128)}, f32[1,256]{1,0:T(1,128)S(1)}, u32[]{:S(2)}, u32[]{:S(2)}) collective-permute-start(f32[1,256]{1,0:T(1,128)} %shard_map.85), channel_id=1, source_target_pairs={{0,1},{1,0},{2,3},{3,2},{4,5},{5,4},{6,7},{7,6},{8,9},{9,8},{10,11... | collective-permute-start | bytes 3080 | tf_op jit(solution)/shard_map/ppermute | solution.py:53
  216.5 4.0 %collective-permute-start.16 = (f32[128]{0:T(128)S(1)}, f32[128]{0:T(128)S(1)}, u32[]{:S(2)}, u32[]{:S(2)}) collective-permute-start(f32[128]{0:T(128)S(1)} %fusion), channel_id=1, source_target_pairs={{0,4},{1,5},{2,6},{3,7},{4,0},{5,1},{6,2},{7,3},{8,12},{9,13},{10,... | collective-permute-start | bytes 1544 | tf_op jit(solution)/shard_map/ppermute | solution.py:53
  220.6 3.9 %collective-permute-start.17 = (f32[128]{0:T(128)S(1)}, f32[128]{0:T(128)S(1)}, u32[]{:S(2)}, u32[]{:S(2)}) collective-permute-start(f32[128]{0:T(128)S(1)} %fusion.1), channel_id=1, source_target_pairs={{0,16},{1,17},{2,18},{3,19},{4,20},{5,21},{6,22},{7,23},{8,24},{9,... | collective-permute-start | bytes 1544 | tf_op jit(solution)/shard_map/ppermute | solution.py:53
  220.6 3.9 %collective-permute-start.18 = (f32[128]{0:T(128)S(1)}, f32[128]{0:T(128)S(1)}, u32[]{:S(2)}, u32[]{:S(2)}) collective-permute-start(f32[128]{0:T(128)S(1)} %fusion.1), channel_id=1, source_target_pairs={{0,8},{1,9},{2,10},{3,11},{4,12},{5,13},{6,14},{7,15},{8,0},{9,1},... | collective-permute-start | bytes 1544 | tf_op jit(solution)/shard_map/ppermute | solution.py:53
  220.6 4.2 %collective-permute-start.19 = (f32[128]{0:T(128)S(1)}, f32[128]{0:T(128)S(1)}, u32[]{:S(2)}, u32[]{:S(2)}) collective-permute-start(f32[128]{0:T(128)S(1)} %fusion.1), channel_id=1, source_target_pairs={{0,24},{1,25},{2,26},{3,27},{4,28},{5,29},{6,30},{7,31},{8,16},{9,... | collective-permute-start | bytes 1544 | tf_op jit(solution)/shard_map/ppermute | solution.py:53
  224.8 3.9 %collective-permute-start.20 = (f32[128]{0:T(128)S(1)}, f32[128]{0:T(128)S(1)}, u32[]{:S(2)}, u32[]{:S(2)}) collective-permute-start(f32[128]{0:T(128)S(1)} %add_add_fusion), channel_id=1, source_target_pairs={{0,64},{1,65},{2,66},{3,67},{4,68},{5,69},{6,70},{7,71},{8,72},{9,... | collective-permute-start | bytes 1544 | tf_op jit(solution)/shard_map/ppermute | solution.py:53
  (7 other events, 52.7 us)
where the time goes:
time: 236 us; the launch traced here: 232 us
  waiting for transfers between devices  104 us (44%)
  starting transfers between devices  62 us (26%)
  Pallas kernels  58.6 us (25%)
  local copies, waits for them, and re-layouts  3.5 us (1%)
  between operations  2.51 us (1%)
    ppermute x23, waiting for transfers between devices, send(): return lax.ppermute(value, AXES, table)  64.4 us
    all_to_all x4, waiting for transfers between devices, exchange(): return lax.all_to_all(rows, 'lat', split_axis=0, concat_axis=0, tiled=True)  39.8 us
    all_to_all x4, starting transfers between devices, exchange(): return lax.all_to_all(rows, 'lat', split_axis=0, concat_axis=0, tiled=True)  37.8 us
    pallas_call x10, Pallas kernels, call(): pl.pallas_call(kernel, in_specs=[smem()] * scalars + [whole()] * (len(arg...  24.5 us
    ppermute x23, starting transfers between devices, send(): return lax.ppermute(value, AXES, table)  24.1 us
    pallas_call x2, Pallas kernels, decode(): pl.pallas_call(kernel, grid=(WIDTH // tile,), in_specs=[smem()] + [whole(...  18.4 us
    pallas_call x2, Pallas kernels, encode(): pl.pallas_call(kernel, grid=(BLOCK // tile,), in_specs=[smem(), whole(),...  15.7 us
  transfers between devices with their start and end apart: 27, of which 16 were waited for; matrix products, arithmetic and copies ran while one was open for 0% of the time, Pallas kernels for 23%

commit v1 on v0

v1 whole, which is shorter than its diff:
```python
import jax
import jax.numpy as jnp
from jax import lax
from jax.experimental import pallas as pl
from jax.experimental.pallas import tpu as pltpu
from jax.sharding import PartitionSpec as P


AXES = ("lat", "tp")
N_Z, N_Y, N_C, N_X = 4, 4, 2, 4
OWNERS = N_Z * N_Y * N_C
TOK = 256
WIDTH = 1792
BLOCK = 2048
SLOTS = 32
CHUNKS = 2
PART = SLOTS // CHUNKS
ROWS = OWNERS * PART
QUARTER = ROWS // N_X
HALVES = 2


def split_index(index):
    x = index % N_X
    lat = index // N_X
    return lat // (N_Y * N_C), (lat // N_C) % N_Y, lat % N_C, x


def pairs(change):
    out = []
    for index in range(N_Z * N_Y * N_C * N_X):
        z, y, c, x = change(*split_index(index))
        out.append((index, ((z * N_Y + y) * N_C + c) * N_X + x))
    return out


def first(c):
    return 1 + 2 * c


def second(c):
    return 3 - 2 * c


TO_XA = pairs(lambda z, y, c, x: (z, y, c, x ^ first(c)))
TO_XB = pairs(lambda z, y, c, x: (z, y, c, x ^ second(c)))
TO_CORE = pairs(lambda z, y, c, x: (z, y, 1 - c, x))
TO_X = [pairs(lambda z, y, c, x, d=d: (z, y, c, x ^ d)) for d in (1, 2, 3)]
TO_Y = [pairs(lambda z, y, c, x, d=d: (z, y ^ d, c, x)) for d in (1, 2, 3)]
TO_Z = [pairs(lambda z, y, c, x, d=d: (z ^ d, y, c, x)) for d in (1, 2, 3)]


def send(value, table):
    return lax.ppermute(value, AXES, table)


def smem():
    return pl.BlockSpec(memory_space=pltpu.SMEM)


def whole():
    return pl.BlockSpec(memory_space=pltpu.VMEM)


def near_core(value):
    return pltpu.with_memory_space_constraint(value, pltpu.VMEM)


def call(kernel, outs, args, flops, local=(), scalars=0):
    moved = sum(a.size * a.dtype.itemsize for a in args) // 4
    args = [near_core(a) if i in local else a for i, a in enumerate(args)]
    return pl.pallas_call(
        kernel,
        in_specs=[smem()] * scalars + [whole()] * (len(args) - scalars),
        out_specs=[whole()] * len(outs),
        out_shape=[jax.ShapeDtypeStruct(shape, dtype) for shape, dtype in outs],
        cost_estimate=pl.CostEstimate(flops=flops, transcendentals=0, bytes_accessed=moved),
    )(*args)


def lane_sums(values):
    acc = values[:, :128]
    for start in range(128, values.shape[1], 128):
        acc = acc + values[:, start:start + 128]
    return jnp.sum(acc.T, axis=0, keepdims=True)


def slot_codes(ids_ref):
    block = lax.broadcasted_iota(jnp.int32, (OWNERS, TOK), 0)
    one0 = jnp.where(ids_ref[0:1, :] == block, 1.0, 0.0)
    one1 = jnp.where(ids_ref[1:2, :] == block, 1.0, 0.0)
    before = lax.broadcasted_iota(jnp.int32, (TOK, TOK), 0) < lax.broadcasted_iota(jnp.int32, (TOK, TOK), 1)
    before = jnp.where(before, 1.0, 0.0).astype(jnp.bfloat16)
    count0 = jnp.dot(one0.astype(jnp.bfloat16), before, preferred_element_type=jnp.float32)
    count1 = jnp.dot(one1.astype(jnp.bfloat16), before, preferred_element_type=jnp.float32)
    count1 = count1 + jnp.sum(one0, axis=1, keepdims=True)
    rank0 = jnp.sum(one0 * count0, axis=0, keepdims=True).astype(jnp.int32)
    rank1 = jnp.sum(one1 * count1, axis=0, keepdims=True).astype(jnp.int32)
    return ids_ref[0:1, :] * SLOTS + rank0, ids_ref[1:2, :] * SLOTS + rank1


def picks(code0, code1, chunk):
    row = lax.broadcasted_iota(jnp.int32, (ROWS, 1), 0)
    want = row // PART * SLOTS + chunk * PART + row % PART
    hit = (code0 == want) | (code1 == want)
    return jnp.where(hit, 1.0, 0.0).astype(jnp.bfloat16)


def packed_rows(values, code0, code1, bias_ref, chunk):
    centred = (values - bias_ref[...].reshape(1, WIDTH)).astype(jnp.bfloat16)
    rows = jnp.dot(picks(code0, code1, chunk), centred, preferred_element_type=jnp.float32)
    return rows.astype(jnp.bfloat16).reshape(OWNERS, PART, WIDTH)


def pack_first(activations, ids, dec_bias):
    def kernel(act_ref, ids_ref, bias_ref, code_ref, out_ref):
        code0, code1 = slot_codes(ids_ref)
        code_ref[0:1, :] = code0
        code_ref[1:2, :] = code1
        out_ref[...] = packed_rows(act_ref[...].astype(jnp.float32), code0, code1, bias_ref, 0)

    outs = [((2, TOK), jnp.int32), ((OWNERS, PART, WIDTH), jnp.bfloat16)]
    return call(kernel, outs, [activations, ids, dec_bias], 2 * ROWS * TOK * WIDTH)


def pack_next(chunk, activations, code, dec_bias):
    def kernel(act_ref, code_ref, bias_ref, out_ref, norm_ref):
        values = act_ref[...].astype(jnp.float32)
        norm_ref[...] = lane_sums(values * values)
        out_ref[...] = packed_rows(values, code_ref[0:1, :], code_ref[1:2, :], bias_ref, chunk)

    outs = [((OWNERS, PART, WIDTH), jnp.bfloat16), ((1, TOK), jnp.float32)]
    return call(kernel, outs, [activations, code, dec_bias], 2 * ROWS * TOK * WIDTH)


def quarters(meta):
    index = meta[0]
    x, c = index % N_X, (index // N_X) % N_C
    return [pl.multiple_of((x ^ d) * QUARTER, QUARTER) for d in (0, second(c), first(c), 2)]


def encode(half, meta, rows, weight, bias, tile=512):
    steps = BLOCK // HALVES // tile

    def kernel(meta_ref, rows_ref, weight_ref, bias_ref, own_ref, near_ref, away_ref, part_ref):
        own, near, away, far = quarters(meta_ref)
        part = jnp.dot(rows_ref[...].reshape(ROWS, WIDTH), weight_ref[...], preferred_element_type=jnp.float32)
        part_ref[...] = part.astype(jnp.bfloat16)
        own_ref[...] = part_ref[pl.ds(own, QUARTER), :].astype(jnp.float32) + bias_ref[...]
        near_ref[...] = part_ref[pl.ds(near, QUARTER), :]
        away_ref[0:QUARTER, :] = part_ref[pl.ds(away, QUARTER), :]
        away_ref[QUARTER:, :] = part_ref[pl.ds(far, QUARTER), :]

    outs = [(QUARTER, jnp.float32), (QUARTER, jnp.bfloat16), (2 * QUARTER, jnp.bfloat16)]
    wide = BLOCK // HALVES
    return pl.pallas_call(
        kernel,
        grid=(steps,),
        in_specs=[
            smem(),
            whole(),
            pl.BlockSpec((WIDTH, tile), lambda j: (0, half * steps + j)),
            pl.BlockSpec((1, tile), lambda j: (0, half * steps + j)),
        ],
        out_specs=[pl.BlockSpec((count, tile), lambda j: (0, j)) for count, _ in outs],
        out_shape=[jax.ShapeDtypeStruct((count, wide), dtype) for count, dtype in outs],
        scratch_shapes=[pltpu.VMEM((ROWS, tile), jnp.bfloat16)],
        cost_estimate=pl.CostEstimate(flops=2 * ROWS * WIDTH * wide, transcendentals=0, bytes_accessed=2 * WIDTH * wide),
        name="encode",
    )(meta, near_core(rows), weight, bias)


def decode(meta, parts, weight, tile=896):
    wide = BLOCK // HALVES

    def kernel(meta_ref, *refs):
        weight_ref, out_ref, rows_ref = refs[4 * HALVES:]

        @pl.when(pl.program_id(0) == 0)
        def _():
            for half in range(HALVES):
                for start, part_ref in zip(quarters(meta_ref), refs[4 * half:4 * half + 4]):
                    rows_ref[pl.ds(start, QUARTER), half * wide:(half + 1) * wide] = part_ref[...]

        rows = jnp.dot(rows_ref[...], weight_ref[...], preferred_element_type=jnp.float32)
        out_ref[...] = rows.astype(jnp.bfloat16).reshape(OWNERS, PART, tile)

    args = []
    for own, *others in parts:
        args += [own] + [near_core(a) for a in others]
    return pl.pallas_call(
        kernel,
        grid=(WIDTH // tile,),
        in_specs=[smem()] + [whole()] * (4 * HALVES) + [pl.BlockSpec((BLOCK, tile), lambda j: (0, j))],
        out_specs=pl.BlockSpec((OWNERS, PART, tile), lambda j: (0, 0, j)),
        out_shape=jax.ShapeDtypeStruct((OWNERS, PART, WIDTH), jnp.bfloat16),
        scratch_shapes=[pltpu.VMEM((ROWS, BLOCK), jnp.bfloat16)],
        cost_estimate=pl.CostEstimate(flops=2 * ROWS * WIDTH * BLOCK, transcendentals=0, bytes_accessed=2 * WIDTH * BLOCK),
        name="decode",
    )(meta, *args, weight)


def collect(chunk, code_ref, rows_ref):
    return lax.dot_general(
        picks(code_ref[0:1, :], code_ref[1:2, :], chunk), rows_ref[...].reshape(ROWS, WIDTH), (((0,), (0,)), ((), ())), preferred_element_type=jnp.float32
    )


def collect_rows(chunk, code, rows, base):
    def kernel(code_ref, rows_ref, base_ref, out_ref):
        out_ref[...] = base_ref[...].reshape(-1, WIDTH) + collect(chunk, code_ref, rows_ref)

    return call(kernel, [((TOK, WIDTH), jnp.float32)], [code, rows, base], 2 * ROWS * TOK * WIDTH)[0]


def finish(chunk, activations, code, rows, base):
    def kernel(act_ref, code_ref, rows_ref, base_ref, out_ref):
        recon = base_ref[...] + collect(chunk, code_ref, rows_ref)
        diff = act_ref[...].astype(jnp.float32) - recon
        out_ref[...] = lane_sums(diff * diff)

    return call(kernel, [((1, TOK), jnp.float32)], [activations, code, rows, base], 2 * ROWS * TOK * WIDTH, local=(2,))[0]


def sum_tp(value):
    one, two, three = (send(value, table) for table in TO_X)
    return (value + two) + (one + three)


def exchange(rows):
    return lax.all_to_all(rows, "lat", split_axis=0, concat_axis=0, tiled=True)


def steps(activations, active_blocks, enc_weight, enc_bias, dec_weight, dec_bias):
    meta = (lax.axis_index("lat") * N_X + lax.axis_index("tp")).astype(jnp.int32).reshape(1)
    enc_row = enc_bias.reshape(1, BLOCK)
    code, first_rows = pack_first(activations, active_blocks.T, dec_bias)
    sent, norm = [first_rows], None
    for n in range(1, CHUNKS):
        rows, norm = pack_next(n, activations, code, dec_bias)
        sent.append(rows)

    def share(half, rows):
        own_part, near_part, away_part = encode(half, meta, rows, enc_weight, enc_row)
        got = send(away_part, TO_XA)
        near_sum = (near_part.astype(jnp.float32) + got[QUARTER:].astype(jnp.float32)).astype(jnp.bfloat16)
        rest = send(near_sum, TO_XB)
        pre = own_part + got[:QUARTER].astype(jnp.float32) + rest.astype(jnp.float32)
        mine = jnp.maximum(pre, 0.0).astype(jnp.bfloat16)
        near = send(mine, TO_XB)
        away = send(mine, TO_XA)
        far = send(near, TO_XA)
        return mine, near, away, far

    back = []
    for n in range(CHUNKS):
        rows = exchange(sent[n])
        parts = [share(half, rows) for half in range(HALVES)]
        rows = decode(meta, parts, dec_weight)
        back.append(exchange(rows))

    norms = sum_tp(norm) + 1e-6
    recon = dec_bias
    for n in range(CHUNKS - 1):
        recon = collect_rows(n, code, back[n], recon)
    partial = finish(CHUNKS - 1, activations, code, back[-1], recon)
    squares = sum_tp(partial)
    token_error = (squares / norms).reshape(TOK)
    total = token_error[:128] + token_error[128:]
    total = total + send(total, TO_CORE)
    for tables in (TO_Y, TO_Z):
        one, two, three = (send(total, table) for table in tables)
        total = (total + two) + (one + three)
    mean_error = jnp.sum(total) / (TOK * OWNERS)
    return (token_error, mean_error)


def solution(mesh):
    in_specs = (P("lat", "tp"), P("lat", None), P("tp", "lat"), P("lat"), P("lat", "tp"), P("tp"))
    out_specs = (P("lat"), P())
    return jax.shard_map(steps, mesh=mesh, in_specs=in_specs, out_specs=out_specs, check_vma=False)
```

time: 236 us -> 222 us (0.941)
  waiting for transfers between devices: 104 us -> 82.8 us
  starting transfers between devices: 62 us -> 77.9 us
  Pallas kernels: 58.6 us -> 49.2 us
  other arithmetic: 1.26 us -> 6.32 us
  local copies, waits for them, and re-layouts: 3.5 us -> 0.04 us
    ppermute x23 -> x33, waiting for transfers between devices: 64.4 us -> 38.1 us  [send(): return lax.ppermute(value, AXES, table)]
    ppermute x23 -> x33, starting transfers between devices: 24.1 us -> 43.4 us  [send(): return lax.ppermute(value, AXES, table)]
    pallas_call x10 -> x4, Pallas kernels: 24.5 us -> 13.2 us  [call(): pl.pallas_call(kernel, in_specs=[smem()] * scalars + [whole()] * (len(arg...]
    convert_element_type x0 -> x8, other arithmetic: none -> 5.02 us  [the longest x4 2.8 us: share(): mine = jnp.maximum(pre, 0.0).astype(jnp.bfloat16)]
    all_to_all x4, waiting for transfers between devices: 39.8 us -> 44.8 us  [exchange(): return lax.all_to_all(rows, 'lat', split_axis=0, concat_axis=0, tiled=True)]
    pallas_call x2 -> x4, Pallas kernels: 15.7 us -> 20.1 us  [encode(): pl.pallas_call(kernel, grid=(steps,), in_specs=[smem(), whole(), pl.Block...]
    all_to_all x4, starting transfers between devices: 37.8 us -> 34.5 us  [exchange(): return lax.all_to_all(rows, 'lat', split_axis=0, concat_axis=0, tiled=True)]
    pallas_call x2, Pallas kernels: 18.4 us -> 15.9 us  [decode(): pl.pallas_call(kernel, grid=(WIDTH // tile,), in_specs=[smem()] + [whole(...]
  transfers between devices with their start and end apart: 27 -> 37, of which waited for: 16 -> 18; matrix products, arithmetic and copies ran while one was open for 0% -> 2% of each run, Pallas kernels for 23% -> 19%
where the time goes in v1:
time: 222 us; the launch traced here: 219 us
  waiting for transfers between devices  82.8 us (37%)
  starting transfers between devices  77.9 us (35%)
  Pallas kernels  49.2 us (22%)
  other arithmetic  6.32 us (3%)
  between operations  2.64 us (1%)
    all_to_all x4, waiting for transfers between devices, exchange(): return lax.all_to_all(rows, 'lat', split_axis=0, concat_axis=0, tiled=True)  44.8 us
    ppermute x33, starting transfers between devices, send(): return lax.ppermute(value, AXES, table)  43.4 us
    ppermute x33, waiting for transfers between devices, send(): return lax.ppermute(value, AXES, table)  38.1 us
    all_to_all x4, starting transfers between devices, exchange(): return lax.all_to_all(rows, 'lat', split_axis=0, concat_axis=0, tiled=True)  34.5 us
    pallas_call x4, Pallas kernels, encode(): pl.pallas_call(kernel, grid=(steps,), in_specs=[smem(), whole(), pl.Block...  20.1 us
    pallas_call x2, Pallas kernels, decode(): pl.pallas_call(kernel, grid=(WIDTH // tile,), in_specs=[smem()] + [whole(...  15.9 us
    pallas_call x4, Pallas kernels, call(): pl.pallas_call(kernel, in_specs=[smem()] * scalars + [whole()] * (len(arg...  13.2 us
  transfers between devices with their start and end apart: 37, of which 18 were waited for; matrix products, arithmetic and copies ran while one was open for 2% of the time, Pallas kernels for 19%

profile of v1, /device:TPU:1, one launch (start us, length us, event | category | flops | bytes accessed | tf_op | source)
XLA Modules:
  0.0 218.9 jit_solution(8914815594389189995)
XLA Ops:
  0.6 3.3 %shard_map.77 = (s32[2,256]{1,0:T(2,128)}, bf16[32,16,1792]{2,1,0:T(8,128)(2,1)}) custom-call(bf16[256,1792]{1,0:T(8,128)(2,1)} %act_ref.5, s32[2,256]{1,0:T(2,128)} %bitcast.13, f32[1792]{0:T(1024)} %base_ref.1), custom_call_target="tpu_custom_call" | custom-call | flops 469762048 | bytes 231680 | tf_op jit(solution)/shard_map/pallas_call | solution.py:72
  3.9 9.6 %all-to-all-start.2 = ((bf16[32,16,1792]{2,1,0:T(8,128)(2,1)}), bf16[32,16,1792]{2,1,0:T(8,128)(2,1)S(1)}, u32[]{:S(2)}, u32[]{:S(2)}) async-start(bf16[32,16,1792]{2,1,0:T(8,128)(2,1)} %get-tuple-element.26), calls=%async_computation.2 | async-start | bytes 3670016 | tf_op jit(solution)/shard_map/all_to_all | solution.py:231
  13.5 25.8 %all-to-all-done.2.rows_ref = bf16[32,16,1792]{2,1,0:T(8,128)(2,1)S(1)} async-done(((bf16[32,16,1792]{2,1,0:T(8,128)(2,1)}), bf16[32,16,1792]{2,1,0:T(8,128)(2,1)S(1)}, u32[]{:S(2)}, u32[]{:S(2)}) %all-to-all-start.2) | async-done | bytes 1835040 | tf_op jit(solution)/shard_map/all_to_all | solution.py:231
  39.4 4.7 %encode.6 = (f32[128,1024]{1,0:T(8,128)}, bf16[128,1024]{1,0:T(8,128)(2,1)}, bf16[256,1024]{1,0:T(8,128)(2,1)}) custom-call(s32[1]{0:T(128)} %bitcast.1.meta_ref, bf16[32,16,1792]{2,1,0:T(8,128)(2,1)S(1)} %all-to-all-done.2.rows_ref, bf16[1792,2048]{1,0:T(8,128)(2,1)} %weight_ref.7, f32[1,2048]{1,0:T(1,128)} %bitcast.8), custom_call_target="tpu_custom_call" | custom-call | flops 1879048192 | bytes 3670016 | tf_op jit(solution)/shard_map/encode/pallas_call | solution.py:156
  44.0 2.5 %collective-permute-start.10 = (bf16[256,1024]{1,0:T(8,128)(2,1)}, bf16[256,1024]{1,0:T(8,128)(2,1)S(1)}, u32[]{:S(2)}, u32[]{:S(2)}) collective-permute-start(bf16[256,1024]{1,0:T(8,128)(2,1)} %get-tuple-element.28), channel_id=1, source_target_pairs={{0,1},{1,0},{2,3},{3,2},{4,7},{5,6},{6,5},{7,4},{8,9},{9,8},{10,11... | collective-permute-start | bytes 1572872 | tf_op jit(solution)/shard_map/ppermute | solution.py:54
  46.5 3.2 %shard_map.78 = (bf16[32,16,1792]{2,1,0:T(8,128)(2,1)}, f32[1,256]{1,0:T(1,128)}) custom-call(bf16[256,1792]{1,0:T(8,128)(2,1)} %act_ref.5, s32[2,256]{1,0:T(2,128)} %get-tuple-element.18.code_ref, f32[1792]{0:T(1024)} %base_ref.1), custom_call_target="tpu_custom_call" | custom-call | flops 469762048 | bytes 231680 | tf_op jit(solution)/shard_map/pallas_call | solution.py:72
  49.7 4.8 %all-to-all-start = ((bf16[32,16,1792]{2,1,0:T(8,128)(2,1)}), bf16[32,16,1792]{2,1,0:T(8,128)(2,1)}, u32[]{:S(2)}, u32[]{:S(2)}) async-start(bf16[32,16,1792]{2,1,0:T(8,128)(2,1)} %get-tuple-element.19), calls=%async_computation | async-start | bytes 3670016 | tf_op jit(solution)/shard_map/all_to_all | solution.py:231
  54.5 4.8 %encode.7 = (f32[128,1024]{1,0:T(8,128)}, bf16[128,1024]{1,0:T(8,128)(2,1)}, bf16[256,1024]{1,0:T(8,128)(2,1)}) custom-call(s32[1]{0:T(128)} %bitcast.1.meta_ref, bf16[32,16,1792]{2,1,0:T(8,128)(2,1)S(1)} %all-to-all-done.2.rows_ref, bf16[1792,2048]{1,0:T(8,128)(2,1)} %weight_ref.7, f32[1,2048]{1,0:T(1,128)} %bitcast.9), custom_call_target="tpu_custom_call" | custom-call | flops 1879048192 | bytes 3670016 | tf_op jit(solution)/shard_map/encode/pallas_call | solution.py:156
  61.7 10.4 %collective-permute-done.15 = bf16[256,1024]{1,0:T(8,128)(2,1)S(1)} collective-permute-done((bf16[256,1024]{1,0:T(8,128)(2,1)}, bf16[256,1024]{1,0:T(8,128)(2,1)S(1)}, u32[]{:S(2)}, u32[]{:S(2)}) %collective-permute-start.15) | collective-permute-done | bytes 524320 | tf_op jit(solution)/shard_map/ppermute | solution.py:54
  75.4 3.2 %collective-permute-done.16 = bf16[128,1024]{1,0:T(8,128)(2,1)S(1)} collective-permute-done((bf16[128,1024]{1,0:T(8,128)(2,1)S(1)}, bf16[128,1024]{1,0:T(8,128)(2,1)S(1)}, u32[]{:S(2)}, u32[]{:S(2)}) %collective-permute-start.16) | collective-permute-done | bytes 262176 | tf_op jit(solution)/shard_map/ppermute | solution.py:54
  86.7 5.3 %encode.5 = (f32[128,1024]{1,0:T(8,128)}, bf16[128,1024]{1,0:T(8,128)(2,1)}, bf16[256,1024]{1,0:T(8,128)(2,1)}) custom-call(s32[1]{0:T(128)} %bitcast.1.meta_ref, bf16[32,16,1792]{2,1,0:T(8,128)(2,1)} %all-to-all-done.rows_ref, bf16[1792,2048]{1,0:T(8,128)(2,1)} %weight_ref.7, f32[1,2048]{1,0:T(1,128)} %bitcast.10), custom_call_target="tpu_custom_call" | custom-call | flops 1879048192 | bytes 3670016 | tf_op jit(solution)/shard_map/encode/pallas_call | solution.py:156
  92.9 5.3 %encode.4 = (f32[128,1024]{1,0:T(8,128)}, bf16[128,1024]{1,0:T(8,128)(2,1)}, bf16[256,1024]{1,0:T(8,128)(2,1)}) custom-call(s32[1]{0:T(128)} %bitcast.1.meta_ref, bf16[32,16,1792]{2,1,0:T(8,128)(2,1)} %all-to-all-done.rows_ref, bf16[1792,2048]{1,0:T(8,128)(2,1)} %weight_ref.7, f32[1,2048]{1,0:T(1,128)} %bitcast.11), custom_call_target="tpu_custom_call" | custom-call | flops 1879048192 | bytes 3670016 | tf_op jit(solution)/shard_map/encode/pallas_call | solution.py:156
  100.1 8.0 %decode.3 = bf16[32,16,1792]{2,1,0:T(8,128)(2,1)} custom-call(s32[1]{0:T(128)} %bitcast.1.meta_ref, bf16[128,1024]{1,0:T(8,128)(2,1)} %maximum_convert_fusion.1.refs_0_, bf16[128,1024]{1,0:T(8,128)(2,1)S(1)} %collective-permute-done.12.refs_1_, bf16[128,1024]{1,0:T(8,128)(2,1)S(1)} %collective-permute-done.13.refs_2_, ...), custom_call_target="tpu_custom_call" | custom-call | flops 3758096384 | bytes 7340032 | tf_op jit(solution)/shard_map/decode/pallas_call | solution.py:191
  108.1 12.0 %all-to-all-start.3 = ((bf16[32,16,1792]{2,1,0:T(8,128)(2,1)}), bf16[32,16,1792]{2,1,0:T(8,128)(2,1)}, u32[]{:S(2)}, u32[]{:S(2)}) async-start(bf16[32,16,1792]{2,1,0:T(8,128)(2,1)} %decode.3), calls=%async_computation.3 | async-start | bytes 3670016 | tf_op jit(solution)/shard_map/all_to_all | solution.py:231
  123.2 4.0 %collective-permute-done.6 = bf16[128,1024]{1,0:T(8,128)(2,1)S(1)} collective-permute-done((bf16[128,1024]{1,0:T(8,128)(2,1)S(1)}, bf16[128,1024]{1,0:T(8,128)(2,1)S(1)}, u32[]{:S(2)}, u32[]{:S(2)}) %collective-permute-start.6) | collective-permute-done | bytes 262176 | tf_op jit(solution)/shard_map/ppermute | solution.py:54
  141.3 5.0 %collective-permute-done.3.refs_2_ = bf16[128,1024]{1,0:T(8,128)(2,1)S(1)} collective-permute-done((bf16[128,1024]{1,0:T(8,128)(2,1)S(1)}, bf16[128,1024]{1,0:T(8,128)(2,1)S(1)}, u32[]{:S(2)}, u32[]{:S(2)}) %collective-permute-start.3) | collective-permute-done | bytes 262176 | tf_op jit(solution)/shard_map/ppermute | solution.py:54
  148.7 2.8 %collective-permute-done.4.refs_3_ = bf16[128,1024]{1,0:T(8,128)(2,1)S(1)} collective-permute-done((bf16[128,1024]{1,0:T(8,128)(2,1)S(1)}, bf16[128,1024]{1,0:T(8,128)(2,1)S(1)}, u32[]{:S(2)}, u32[]{:S(2)}) %collective-permute-start.4) | collective-permute-done | bytes 262176 | tf_op jit(solution)/shard_map/ppermute | solution.py:54
  151.5 7.9 %decode.2 = bf16[32,16,1792]{2,1,0:T(8,128)(2,1)} custom-call(s32[1]{0:T(128)} %bitcast.1.meta_ref, bf16[128,1024]{1,0:T(8,128)(2,1)} %copy-done.7, bf16[128,1024]{1,0:T(8,128)(2,1)S(1)} %collective-permute-done.2.refs_1_, bf16[128,1024]{1,0:T(8,128)(2,1)S(1)} %collective-permute-done.3.refs_2_, bf16[128,1024]{1,0:T(8,128)(2,1)S(1)} %collective-permute-done.4.refs_3_, ...), custom_call_target="tpu_custom_call" | custom-call | flops 3758096384 | bytes 7340032 | tf_op jit(solution)/shard_map/decode/pallas_call | solution.py:191
  159.4 8.1 %all-to-all-start.1 = ((bf16[32,16,1792]{2,1,0:T(8,128)(2,1)}), bf16[32,16,1792]{2,1,0:T(8,128)(2,1)S(1)}, u32[]{:S(2)}, u32[]{:S(2)}) async-start(bf16[32,16,1792]{2,1,0:T(8,128)(2,1)} %decode.2), calls=%async_computation.1 | async-start | bytes 3670016 | tf_op jit(solution)/shard_map/all_to_all | solution.py:231
  170.8 3.5 %shard_map.79.base_ref = f32[256,1792]{1,0:T(8,128)} custom-call(s32[2,256]{1,0:T(2,128)} %get-tuple-element.18.code_ref, bf16[32,16,1792]{2,1,0:T(8,128)(2,1)} %all-to-all-done.3.rows_ref, f32[1792]{0:T(1024)} %base_ref.1), custom_call_target="tpu_custom_call" | custom-call | flops 469762048 | bytes 461056 | tf_op jit(solution)/shard_map/pallas_call | solution.py:72
  174.4 19.0 %all-to-all-done.1.rows_ref = bf16[32,16,1792]{2,1,0:T(8,128)(2,1)S(1)} async-done(((bf16[32,16,1792]{2,1,0:T(8,128)(2,1)}), bf16[32,16,1792]{2,1,0:T(8,128)(2,1)S(1)}, u32[]{:S(2)}, u32[]{:S(2)}) %all-to-all-start.1) | async-done | bytes 1835040 | tf_op jit(solution)/shard_map/all_to_all | solution.py:231
  193.3 3.2 %shard_map.80 = f32[1,256]{1,0:T(1,128)} custom-call(bf16[256,1792]{1,0:T(8,128)(2,1)} %act_ref.5, s32[2,256]{1,0:T(2,128)} %get-tuple-element.18.code_ref, bf16[32,16,1792]{2,1,0:T(8,128)(2,1)S(1)} %all-to-all-done.1.rows_ref, f32[256,1792]{1,0:T(8,128)} %shard_map.79.base_ref), custom_call_target="tpu_custom_call" | custom-call | flops 469762048 | bytes 1147392 | tf_op jit(solution)/shard_map/pallas_call | solution.py:72
  203.6 3.1 %collective-permute-start.26 = (f32[128]{0:T(128)S(1)}, f32[128]{0:T(128)S(1)}, u32[]{:S(2)}, u32[]{:S(2)}) collective-permute-start(f32[128]{0:T(128)S(1)} %fusion), channel_id=1, source_target_pairs={{0,4},{1,5},{2,6},{3,7},{4,0},{5,1},{6,2},{7,3},{8,12},{9,13},{10,... | collective-permute-start | bytes 1544 | tf_op jit(solution)/shard_map/ppermute | solution.py:54
  207.5 3.2 %collective-permute-start.29 = (f32[128]{0:T(128)S(1)}, f32[128]{0:T(128)S(1)}, u32[]{:S(2)}, u32[]{:S(2)}) collective-permute-start(f32[128]{0:T(128)S(1)} %fusion.1), channel_id=1, source_target_pairs={{0,24},{1,25},{2,26},{3,27},{4,28},{5,29},{6,30},{7,31},{8,16},{9,... | collective-permute-start | bytes 1544 | tf_op jit(solution)/shard_map/ppermute | solution.py:54
  (95 shorter events, 53.7 us)
Async XLA Ops:
  3.9 35.4 %all-to-all-start.2 = ((bf16[32,16,1792]{2,1,0:T(8,128)(2,1)}), bf16[32,16,1792]{2,1,0:T(8,128)(2,1)S(1)}, u32[]{:S(2)}, u32[]{:S(2)}) async-start(bf16[32,16,1792]{2,1,0:T(8,128)(2,1)} %get-tuple-element.26), calls=%async_computation.2 | async-start | bytes 3670016 | tf_op jit(solution)/shard_map/all_to_all | solution.py:231
  44.0 17.1 %collective-permute-start.10 = (bf16[256,1024]{1,0:T(8,128)(2,1)}, bf16[256,1024]{1,0:T(8,128)(2,1)S(1)}, u32[]{:S(2)}, u32[]{:S(2)}) collective-permute-start(bf16[256,1024]{1,0:T(8,128)(2,1)} %get-tuple-element.28), channel_id=1, source_target_pairs={{0,1},{1,0},{2,3},{3,2},{4,7},{5,6},{6,5},{7,4},{8,9},{9,8},{10,11... | collective-permute-start | bytes 1572872 | tf_op jit(solution)/shard_map/ppermute | solution.py:54
  49.7 37.0 %all-to-all-start = ((bf16[32,16,1792]{2,1,0:T(8,128)(2,1)}), bf16[32,16,1792]{2,1,0:T(8,128)(2,1)}, u32[]{:S(2)}, u32[]{:S(2)}) async-start(bf16[32,16,1792]{2,1,0:T(8,128)(2,1)} %get-tuple-element.19), calls=%async_computation | async-start | bytes 3670016 | tf_op jit(solution)/shard_map/all_to_all | solution.py:231
  59.3 12.7 %collective-permute-start.15 = (bf16[256,1024]{1,0:T(8,128)(2,1)}, bf16[256,1024]{1,0:T(8,128)(2,1)S(1)}, u32[]{:S(2)}, u32[]{:S(2)}) collective-permute-start(bf16[256,1024]{1,0:T(8,128)(2,1)} %get-tuple-element.31), channel_id=1, source_target_pairs={{0,1},{1,0},{2,3},{3,2},{4,7},{5,6},{6,5},{7,4},{8,9},{9,8},{10,11... | collective-permute-start | bytes 1572872 | tf_op jit(solution)/shard_map/ppermute | solution.py:54
  61.3 11.9 %collective-permute-start.11 = (bf16[128,1024]{1,0:T(8,128)(2,1)S(1)}, bf16[128,1024]{1,0:T(8,128)(2,1)S(1)}, u32[]{:S(2)}, u32[]{:S(2)}) collective-permute-start(bf16[128,1024]{1,0:T(8,128)(2,1)S(1)} %add_convert_fusion.1), channel_id=1, source_target_pairs={{0,3},{1,2},{2,1},{3,0},{4,5},{5,4},{6,7},{7,6},{8,11},{9,10},{10,... | collective-permute-start | bytes 786440 | tf_op jit(solution)/shard_map/ppermute | solution.py:54
  74.0 8.1 %collective-permute-start.12 = (bf16[128,1024]{1,0:T(8,128)(2,1)}, bf16[128,1024]{1,0:T(8,128)(2,1)S(1)}, u32[]{:S(2)}, u32[]{:S(2)}) collective-permute-start(bf16[128,1024]{1,0:T(8,128)(2,1)} %maximum_convert_fusion.1.refs_0_), channel_id=1, source_target_pairs={{0,3},{1,2},{2,1},{3,0},{4,5},{5,4},{6,7},{7,6},{8,11},{9,10},{10,... | collective-permute-start | bytes 786440 | tf_op jit(solution)/shard_map/ppermute | solution.py:54
  79.5 18.7 %collective-permute-start.13 = (bf16[128,1024]{1,0:T(8,128)(2,1)}, bf16[128,1024]{1,0:T(8,128)(2,1)S(1)}, u32[]{:S(2)}, u32[]{:S(2)}) collective-permute-start(bf16[128,1024]{1,0:T(8,128)(2,1)} %maximum_convert_fusion.1.refs_0_), channel_id=1, source_target_pairs={{0,1},{1,0},{2,3},{3,2},{4,7},{5,6},{6,5},{7,4},{8,9},{9,8},{10,11... | collective-permute-start | bytes 786440 | tf_op jit(solution)/shard_map/ppermute | solution.py:54
  81.3 18.8 %collective-permute-start.18 = (bf16[128,1024]{1,0:T(8,128)(2,1)}, bf16[128,1024]{1,0:T(8,128)(2,1)S(1)}, u32[]{:S(2)}, u32[]{:S(2)}) collective-permute-start(bf16[128,1024]{1,0:T(8,128)(2,1)} %maximum_convert_fusion.refs_4_), channel_id=1, source_target_pairs={{0,1},{1,0},{2,3},{3,2},{4,7},{5,6},{6,5},{7,4},{8,9},{9,8},{10,11... | collective-permute-start | bytes 786440 | tf_op jit(solution)/shard_map/ppermute | solution.py:54
  82.1 17.9 %collective-permute-start.14 = (bf16[128,1024]{1,0:T(8,128)(2,1)S(1)}, bf16[128,1024]{1,0:T(8,128)(2,1)S(1)}, u32[]{:S(2)}, u32[]{:S(2)}) collective-permute-start(bf16[128,1024]{1,0:T(8,128)(2,1)S(1)} %collective-permute-done.12.refs_1_), channel_id=1, source_target_pairs={{0,1},{1,0},{2,3},{3,2},{4,7},{5,6},{6,5},{7,4},{8,9},{9,8},{10,11... | collective-permute-start | bytes 786440 | tf_op jit(solution)/shard_map/ppermute | solution.py:54
  84.9 15.2 %collective-permute-start.19 = (bf16[128,1024]{1,0:T(8,128)(2,1)S(1)}, bf16[128,1024]{1,0:T(8,128)(2,1)S(1)}, u32[]{:S(2)}, u32[]{:S(2)}) collective-permute-start(bf16[128,1024]{1,0:T(8,128)(2,1)S(1)} %collective-permute-done.17.refs_5_), channel_id=1, source_target_pairs={{0,1},{1,0},{2,3},{3,2},{4,7},{5,6},{6,5},{7,4},{8,9},{9,8},{10,11... | collective-permute-start | bytes 786440 | tf_op jit(solution)/shard_map/ppermute | solution.py:54
  92.0 28.1 %collective-permute-start.5 = (bf16[256,1024]{1,0:T(8,128)(2,1)}, bf16[256,1024]{1,0:T(8,128)(2,1)}, u32[]{:S(2)}, u32[]{:S(2)}) collective-permute-start(bf16[256,1024]{1,0:T(8,128)(2,1)} %get-tuple-element.24), channel_id=1, source_target_pairs={{0,1},{1,0},{2,3},{3,2},{4,7},{5,6},{6,5},{7,4},{8,9},{9,8},{10,11... | collective-permute-start | bytes 1572872 | tf_op jit(solution)/shard_map/ppermute | solution.py:54
  98.1 24.9 %collective-permute-start = (bf16[256,1024]{1,0:T(8,128)(2,1)}, bf16[256,1024]{1,0:T(8,128)(2,1)S(1)}, u32[]{:S(2)}, u32[]{:S(2)}) collective-permute-start(bf16[256,1024]{1,0:T(8,128)(2,1)} %get-tuple-element.21), channel_id=1, source_target_pairs={{0,1},{1,0},{2,3},{3,2},{4,7},{5,6},{6,5},{7,4},{8,9},{9,8},{10,11... | collective-permute-start | bytes 1572872 | tf_op jit(solution)/shard_map/ppermute | solution.py:54
  108.1 51.3 %all-to-all-start.3 = ((bf16[32,16,1792]{2,1,0:T(8,128)(2,1)}), bf16[32,16,1792]{2,1,0:T(8,128)(2,1)}, u32[]{:S(2)}, u32[]{:S(2)}) async-start(bf16[32,16,1792]{2,1,0:T(8,128)(2,1)} %decode.3), calls=%async_computation.3 | async-start | bytes 3670016 | tf_op jit(solution)/shard_map/all_to_all | solution.py:231
  123.1 6.9 %collective-permute-start.1 = (bf16[128,1024]{1,0:T(8,128)(2,1)S(1)}, bf16[128,1024]{1,0:T(8,128)(2,1)S(1)}, u32[]{:S(2)}, u32[]{:S(2)}) collective-permute-start(bf16[128,1024]{1,0:T(8,128)(2,1)S(1)} %add_convert_fusion.3), channel_id=1, source_target_pairs={{0,3},{1,2},{2,1},{3,0},{4,5},{5,4},{6,7},{7,6},{8,11},{9,10},{10,... | collective-permute-start | bytes 786440 | tf_op jit(solution)/shard_map/ppermute | solution.py:54
  128.2 6.1 %collective-permute-start.7 = (bf16[128,1024]{1,0:T(8,128)(2,1)S(1)}, bf16[128,1024]{1,0:T(8,128)(2,1)S(1)}, u32[]{:S(2)}, u32[]{:S(2)}) collective-permute-start(bf16[128,1024]{1,0:T(8,128)(2,1)S(1)} %maximum_convert_fusion.2.refs_4_), channel_id=1, source_target_pairs={{0,3},{1,2},{2,1},{3,0},{4,5},{5,4},{6,7},{7,6},{8,11},{9,10},{10,... | collective-permute-start | bytes 786440 | tf_op jit(solution)/shard_map/ppermute | solution.py:54
  130.1 7.0 %collective-permute-start.2 = (bf16[128,1024]{1,0:T(8,128)(2,1)S(1)}, bf16[128,1024]{1,0:T(8,128)(2,1)S(1)}, u32[]{:S(2)}, u32[]{:S(2)}) collective-permute-start(bf16[128,1024]{1,0:T(8,128)(2,1)S(1)} %maximum_convert_fusion.3.refs_0_), channel_id=1, source_target_pairs={{0,3},{1,2},{2,1},{3,0},{4,5},{5,4},{6,7},{7,6},{8,11},{9,10},{10,... | collective-permute-start | bytes 786440 | tf_op jit(solution)/shard_map/ppermute | solution.py:54
  131.6 9.6 %collective-permute-start.8 = (bf16[128,1024]{1,0:T(8,128)(2,1)S(1)}, bf16[128,1024]{1,0:T(8,128)(2,1)S(1)}, u32[]{:S(2)}, u32[]{:S(2)}) collective-permute-start(bf16[128,1024]{1,0:T(8,128)(2,1)S(1)} %maximum_convert_fusion.2.refs_4_), channel_id=1, source_target_pairs={{0,1},{1,0},{2,3},{3,2},{4,7},{5,6},{6,5},{7,4},{8,9},{9,8},{10,11... | collective-permute-start | bytes 786440 | tf_op jit(solution)/shard_map/ppermute | solution.py:54
  133.4 12.8 %collective-permute-start.3 = (bf16[128,1024]{1,0:T(8,128)(2,1)S(1)}, bf16[128,1024]{1,0:T(8,128)(2,1)S(1)}, u32[]{:S(2)}, u32[]{:S(2)}) collective-permute-start(bf16[128,1024]{1,0:T(8,128)(2,1)S(1)} %maximum_convert_fusion.3.refs_0_), channel_id=1, source_target_pairs={{0,1},{1,0},{2,3},{3,2},{4,7},{5,6},{6,5},{7,4},{8,9},{9,8},{10,11... | collective-permute-start | bytes 786440 | tf_op jit(solution)/shard_map/ppermute | solution.py:54
  134.3 14.3 %collective-permute-start.9 = (bf16[128,1024]{1,0:T(8,128)(2,1)S(1)}, bf16[128,1024]{1,0:T(8,128)(2,1)S(1)}, u32[]{:S(2)}, u32[]{:S(2)}) collective-permute-start(bf16[128,1024]{1,0:T(8,128)(2,1)S(1)} %collective-permute-done.7.refs_5_), channel_id=1, source_target_pairs={{0,1},{1,0},{2,3},{3,2},{4,7},{5,6},{6,5},{7,4},{8,9},{9,8},{10,11... | collective-permute-start | bytes 786440 | tf_op jit(solution)/shard_map/ppermute | solution.py:54
  137.1 14.4 %collective-permute-start.4 = (bf16[128,1024]{1,0:T(8,128)(2,1)S(1)}, bf16[128,1024]{1,0:T(8,128)(2,1)S(1)}, u32[]{:S(2)}, u32[]{:S(2)}) collective-permute-start(bf16[128,1024]{1,0:T(8,128)(2,1)S(1)} %collective-permute-done.2.refs_1_), channel_id=1, source_target_pairs={{0,1},{1,0},{2,3},{3,2},{4,7},{5,6},{6,5},{7,4},{8,9},{9,8},{10,11... | collective-permute-start | bytes 786440 | tf_op jit(solution)/shard_map/ppermute | solution.py:54
  159.4 33.9 %all-to-all-start.1 = ((bf16[32,16,1792]{2,1,0:T(8,128)(2,1)}), bf16[32,16,1792]{2,1,0:T(8,128)(2,1)S(1)}, u32[]{:S(2)}, u32[]{:S(2)}) async-start(bf16[32,16,1792]{2,1,0:T(8,128)(2,1)} %decode.2), calls=%async_computation.1 | async-start | bytes 3670016 | tf_op jit(solution)/shard_map/all_to_all | solution.py:231
  167.5 31.4 %collective-permute-start.23 = (f32[1,256]{1,0:T(1,128)S(1)}, f32[1,256]{1,0:T(1,128)S(1)}, u32[]{:S(2)}, u32[]{:S(2)}) collective-permute-start(f32[1,256]{1,0:T(1,128)S(1)} %copy-done.10), channel_id=1, source_target_pairs={{0,2},{1,3},{2,0},{3,1},{4,6},{5,7},{6,4},{7,5},{8,10},{9,11},{10,... | collective-permute-start | bytes 3080 | tf_op jit(solution)/shard_map/ppermute | solution.py:54
  168.8 31.0 %collective-permute-start.24 = (f32[1,256]{1,0:T(1,128)S(1)}, f32[1,256]{1,0:T(1,128)S(1)}, u32[]{:S(2)}, u32[]{:S(2)}) collective-permute-start(f32[1,256]{1,0:T(1,128)S(1)} %copy-done.10), channel_id=1, source_target_pairs={{0,1},{1,0},{2,3},{3,2},{4,5},{5,4},{6,7},{7,6},{8,9},{9,8},{10,11... | collective-permute-start | bytes 3080 | tf_op jit(solution)/shard_map/ppermute | solution.py:54
  169.9 29.8 %collective-permute-start.25 = (f32[1,256]{1,0:T(1,128)S(1)}, f32[1,256]{1,0:T(1,128)S(1)}, u32[]{:S(2)}, u32[]{:S(2)}) collective-permute-start(f32[1,256]{1,0:T(1,128)S(1)} %copy-done.10), channel_id=1, source_target_pairs={{0,3},{1,2},{2,1},{3,0},{4,7},{5,6},{6,5},{7,4},{8,11},{9,10},{10,... | collective-permute-start | bytes 3080 | tf_op jit(solution)/shard_map/ppermute | solution.py:54
  (24 other events, 217.6 us)
